TPU v7x, 128 devices: a whole 4x4x4 slice. The times are simulated.
128 devices in a mesh: ctx: 16 (over y, z_hi, core), ch: 2 (over z_lo), dp: 4 (over x).
Axes of the slice: x: 4, y: 4, z: 4 (z_hi: 2, z_lo: 2; z = z_hi * 2 + z_lo), core: 2. Of those that a mesh axis runs over, the one named last changes fastest.
Arguments:
- features: bfloat16 [32768, 3, 4096], P(('dp', 'ctx'), None, 'ch'), parts along dimension 0, may hold values from -6 to 6
- short_filter: float32 [3, 3, 4096], P(None, None, 'ch'), may hold values from -3.5 to 3.5
- mode_residue: float32 [16, 4096], P(None, 'ch'), may hold values from -0.18 to 0.18
- decay_mix: float32 [16, 4096], P(None, 'ch'), may hold values from 0 to 1
- skip_gain: float32 [4096], P('ch'), may hold values from 0.5 to 1.5
- counter: int32 [8], P('dp'), parts along dimension 0, may hold values from 0 to 1048575
- out_weight: bfloat16 [4096, 4096], P('ch'), may hold values from -0.09375 to 0.09375
Outputs:
- projected: bfloat16 [32768, 4096], P(('dp', 'ctx', 'ch')), parts along dimension 0
There are 4 independent parts, one for each index of `dp`. A program takes and returns all parts, laid end to end along the dimension named above; an argument that names none is the same for every part. Nothing has to cross between parts.
All inputs are finite; a program needn't handle non-finite values.
Results may differ from a plain program's by a relative error of at most 0.012.
Values may be sent and summed in bfloat16 or wider, within the bound.
No kernel may reach another device: no remote copies, remote signals or barrier semaphores. Data moves between devices by JAX's collectives and lax.ppermute only.
A program may use at most 256 MiB of HBM per device.

v0:
```python
import math
import jax
import jax.numpy as jnp
from jax import lax
from jax.sharding import PartitionSpec as P

SHORT = 3
keep_scale = 8.0 / 7.0
precise = lax.Precision.HIGHEST


def passed_along(value, axis, steps):
    count = lax.axis_size(axis)
    leading, last = (max(0, -steps), min(count, count - steps))
    return lax.ppermute(value, axis, [(source, source + steps) for source in range(leading, last)])


def keep_mask(hash_base, positions, channels):
    bits = (
        hash_base
        + positions[:, None] * jnp.int32(-1640531535)
        + channels[None, :] * jnp.int32(-2048144777)
    )
    bits = bits ^ lax.shift_right_logical(bits, jnp.full_like(bits, 16))
    bits = bits * jnp.int32(2146121005)
    bits = bits ^ lax.shift_right_logical(bits, jnp.full_like(bits, 15))
    bits = bits * jnp.int32(-2073254261)
    bits = bits ^ lax.shift_right_logical(bits, jnp.full_like(bits, 16))
    return lax.shift_right_logical(bits, jnp.full_like(bits, 29)) != 0


def rates_of(mix, length):
    return jnp.exp(-((1.0 - mix) * math.log(length) + mix * math.log(30.0)))


def contract(form, left, right):
    return jnp.einsum(form, left, right, precision=precise)


def trig_table(rows, cols, period):
    product = (
        jnp.arange(rows, dtype=jnp.int32)[:, None]
        * jnp.arange(cols, dtype=jnp.int32)[None, :]
        % period
    )
    angle = product.astype(jnp.float32) * (2.0 * math.pi / period)
    return (jnp.cos(angle), jnp.sin(angle))


def split_table(table):
    upper = table.astype(jnp.bfloat16)
    lower = (table - upper.astype(jnp.float32)).astype(jnp.bfloat16)
    return (upper, lower)


def narrow_section(table, grid):
    upper, lower = split_table(table)
    first = jnp.einsum("ka,abc->kbc", upper, grid, preferred_element_type=jnp.float32)
    return first + jnp.einsum("ka,abc->kbc", lower, grid, preferred_element_type=jnp.float32)


def forward_dft(grid, tables):
    cos_outer, sin_outer, twist_cos, twist_sin, cos_inner, sin_inner = tables
    first_real = narrow_section(cos_outer, grid)
    first_imag = -narrow_section(sin_outer, grid)
    turned_real = first_real * twist_cos[:, :, None] + first_imag * twist_sin[:, :, None]
    turned_imag = first_imag * twist_cos[:, :, None] - first_real * twist_sin[:, :, None]
    out_real = contract("kbc,bm->kmc", turned_real, cos_inner) + contract(
        "kbc,bm->kmc", turned_imag, sin_inner
    )
    out_imag = contract("kbc,bm->kmc", turned_imag, cos_inner) - contract(
        "kbc,bm->kmc", turned_real, sin_inner
    )
    return (out_real, out_imag)


def inverse_dft(spec_real, spec_imag, tables):
    cos_outer, sin_outer, twist_cos, twist_sin, cos_inner, sin_inner = tables
    back_real = contract("kmc,bm->kbc", spec_real, cos_inner) - contract(
        "kmc,bm->kbc", spec_imag, sin_inner
    )
    back_imag = contract("kmc,bm->kbc", spec_imag, cos_inner) + contract(
        "kmc,bm->kbc", spec_real, sin_inner
    )
    turned_real = back_real * twist_cos[:, :, None] - back_imag * twist_sin[:, :, None]
    turned_imag = back_imag * twist_cos[:, :, None] + back_real * twist_sin[:, :, None]
    return contract("ka,kbc->abc", cos_outer, turned_real) - contract(
        "ka,kbc->abc", sin_outer, turned_imag
    )


def filter_spectrum(residue, mix, length, outer_len, inner_len):
    total_len = 2 * length
    rates = rates_of(mix, length)
    freq = (
        jnp.arange(outer_len, dtype=jnp.int32)[:, None]
        + outer_len * jnp.arange(inner_len, dtype=jnp.int32)[None, :]
    )
    angle = freq.astype(jnp.float32) * (2.0 * math.pi / total_len)
    sine_full = jnp.sin(angle)[:, :, None]
    sine_half = jnp.sin(0.5 * angle)[:, :, None]
    parity = (1 - 2 * (freq % 2)).astype(jnp.float32)[:, :, None]
    width = residue.shape[1]

    def add_mode(order_index, totals):
        rate = rates[order_index][None, None, :]
        factor = jnp.exp(-rate)
        numer = 1.0 - parity * jnp.exp(-rate * length)
        denom_real = -jnp.expm1(-rate) + factor * 2.0 * sine_half * sine_half
        denom_imag = factor * sine_full
        scale = (
            residue[order_index][None, None, :]
            * numer
            / (denom_real * denom_real + denom_imag * denom_imag)
        )
        return (totals[0] + scale * denom_real, totals[1] - scale * denom_imag)

    empty = jnp.zeros((outer_len, inner_len, width), jnp.float32)
    return lax.fori_loop(0, residue.shape[0], add_mode, (empty, empty))


def causal_fft(signal, residue, mix):
    length, width = signal.shape
    total_len = 2 * length
    inner_len = 128
    outer_len = total_len // inner_len
    half_outer = outer_len // 2
    cos_outer, sin_outer = trig_table(outer_len, half_outer, outer_len)
    twist_cos, twist_sin = trig_table(outer_len, inner_len, total_len)
    cos_inner, sin_inner = trig_table(inner_len, inner_len, inner_len)
    tables = (cos_outer, sin_outer, twist_cos, twist_sin, cos_inner, sin_inner)
    sig_real, sig_imag = forward_dft(signal.reshape(half_outer, inner_len, width), tables)
    tap_real, tap_imag = filter_spectrum(residue, mix, length, outer_len, inner_len)
    prod_real = sig_real * tap_real - sig_imag * tap_imag
    prod_imag = sig_real * tap_imag + sig_imag * tap_real
    return inverse_dft(prod_real, prod_imag, tables).reshape(length, width) / total_len


def body(features, short_filter, mode_residue, decay_mix, skip_gain, counter, out_weight):
    tok_rows = features.shape[0]
    local_width = features.shape[2]
    ctx_count = lax.axis_size("ctx")
    ctx_index = lax.axis_index("ctx")
    ch_index = lax.axis_index("ch")
    edge = passed_along(features[tok_rows - (SHORT - 1) :], "ctx", 1)
    joined = jnp.concatenate([edge, features], axis=0).astype(jnp.float32)
    filtered = jnp.zeros((tok_rows, 3, local_width), jnp.float32)
    for lag in range(SHORT):
        filtered = (
            filtered
            + short_filter[:, lag, :][None] * joined[SHORT - 1 - lag : SHORT - 1 - lag + tok_rows]
        )
    query = filtered[:, 0]
    keyed = filtered[:, 1]
    valued = filtered[:, 2]
    positions = counter[1] + ctx_index * tok_rows + jnp.arange(tok_rows, dtype=jnp.int32)
    channels = ch_index * local_width + jnp.arange(local_width, dtype=jnp.int32)
    gated = jnp.where(
        keep_mask(counter[0], positions, channels), keyed * valued * keep_scale, 0.0
    ).astype(jnp.bfloat16)
    gated_wide = gated.astype(jnp.float32)
    col_width = local_width // ctx_count
    columns = lax.all_to_all(gated, "ctx", split_axis=1, concat_axis=0, tiled=True)
    residue_part = lax.dynamic_slice_in_dim(mode_residue, ctx_index * col_width, col_width, 1)
    mix_part = lax.dynamic_slice_in_dim(decay_mix, ctx_index * col_width, col_width, 1)
    convolved = causal_fft(columns, residue_part, mix_part)
    conv_out = lax.all_to_all(convolved, "ctx", split_axis=0, concat_axis=1, tiled=True)
    long_out = conv_out + skip_gain[None, :] * gated_wide
    mixed = (query * long_out).astype(jnp.bfloat16)
    return lax.psum_scatter(
        jnp.dot(mixed, out_weight, preferred_element_type=jnp.float32).astype(jnp.bfloat16),
        "ch",
        scatter_dimension=0,
        tiled=True,
    )


def solution(mesh):
    placed = (
        P(("dp", "ctx"), None, "ch"),
        P(None, None, "ch"),
        P(None, "ch"),
        P(None, "ch"),
        P("ch"),
        P("dp"),
        P("ch", None),
    )
    return jax.shard_map(
        body, mesh=mesh, in_specs=placed, out_specs=P(("dp", "ctx", "ch"), None), check_vma=False
    )
```

profile of v0, /device:TPU:1, one launch (start us, length us, event | category | flops | bytes accessed | tf_op | source)
XLA Modules:
  0.0 655.3 jit_solution(195904797394615386)
XLA Ops:
  28.5 11.6 %maximum_convert_fusion = f32[514,3,2048]{0,2,1:T(8,128)} fusion(bf16[512,3,2048]{0,2,1:T(8,128)(2,1)} %copy.65, bf16[2,3,2048]{0,2,1:T(8,128)(2,1)S(1)} %copy.64), kind=kLoop, calls=%fused_computation.62 | loop fusion | flops 12632064 | bytes 18948096 | tf_op jit(solution)/shard_map/convert_element_type | solution.py:146
  40.1 17.3 %fusion.17 = f32[512,3,2048]{0,2,1:T(8,128)S(1)} fusion(f32[514,3,2048]{0,2,1:T(8,128)} %maximum_convert_fusion, f32[3,2048]{1,0:T(4,128)S(1)} %get-tuple-element.271, f32[3,2048]{1,0:T(4,128)S(1)} %get-tuple-element.272, f32[3,2048]{1,0:T(4,128)S(1)} %bitcast.149), kind=kLoop, calls=%fused_computation.31 | loop fusion | flops 15728640 | bytes 50405376 | tf_op jit(solution)/shard_map/add | solution.py:150
  70.9 199.9 %while.19 = (s32[]{:T(128)}, f32[128,128,128]{2,1,0:T(8,128)}, f32[128,128,128]{2,1,0:T(8,128)}, f32[16,128]{1,0:T(8,128)S(1)}, f32[16,128]{1,0:T(8,128)S(1)}, /*index=5*/s32[128]{0:T(128)S(1)}, s32[]{:T(128)}, s32[]{:T(128)}) while((s32[]{:T(128)}, f32[128,128,128]{2,1,0:T(8,128)}, ...), condition=%wide.region_1.2_spmd.clone.clone.clone.clone, body=%wide.region_0.1_spmd.clone.clone.clone.clone.sunk | while | flops 35963392 | bytes 33956460 | solution.py:119
  71.4 9.4 %fusion.188 = (f32[128,128,128]{2,1,0:T(8,128)}, f32[128,128,128]{2,1,0:T(8,128)}) fusion(f32[128,128,128]{2,1,0:T(8,128)} %get-tuple-element.340, f32[128,128]{1,0:T(8,128)S(1)} %get-tuple-element.321, f32[128]{0:T(128)S(1)} %get-tuple-element.323, f32[128,128]{1,0:T(8,128)S(1)} %get-tuple-element.324, f32[128]{0:T(128)S(1)} %broadcast_multiply_fusion.2, ...), kind=kLoop, calls=%fused_computation.7.clone.1 | loop fusion | flops 35651584 | bytes 33753600 | tf_op jit(solution)/shard_map/while/body/eval_jaxpr/sub | solution.py:116
  81.4 12.1 %fusion.188 = (f32[128,128,128]{2,1,0:T(8,128)}, f32[128,128,128]{2,1,0:T(8,128)}) fusion(f32[128,128,128]{2,1,0:T(8,128)} %get-tuple-element.340, f32[128,128]{1,0:T(8,128)S(1)} %get-tuple-element.321, f32[128]{0:T(128)S(1)} %get-tuple-element.323, f32[128,128]{1,0:T(8,128)S(1)} %get-tuple-element.324, f32[128]{0:T(128)S(1)} %broadcast_multiply_fusion.2, ...), kind=kLoop, calls=%fused_computation.7.clone.1 | loop fusion | flops 35651584 | bytes 33753600 | tf_op jit(solution)/shard_map/while/body/eval_jaxpr/sub | solution.py:116
  94.1 12.1 %fusion.188 = (f32[128,128,128]{2,1,0:T(8,128)}, f32[128,128,128]{2,1,0:T(8,128)}) fusion(f32[128,128,128]{2,1,0:T(8,128)} %get-tuple-element.340, f32[128,128]{1,0:T(8,128)S(1)} %get-tuple-element.321, f32[128]{0:T(128)S(1)} %get-tuple-element.323, f32[128,128]{1,0:T(8,128)S(1)} %get-tuple-element.324, f32[128]{0:T(128)S(1)} %broadcast_multiply_fusion.2, ...), kind=kLoop, calls=%fused_computation.7.clone.1 | loop fusion | flops 35651584 | bytes 33753600 | tf_op jit(solution)/shard_map/while/body/eval_jaxpr/sub | solution.py:116
  106.8 12.1 %fusion.188 = (f32[128,128,128]{2,1,0:T(8,128)}, f32[128,128,128]{2,1,0:T(8,128)}) fusion(f32[128,128,128]{2,1,0:T(8,128)} %get-tuple-element.340, f32[128,128]{1,0:T(8,128)S(1)} %get-tuple-element.321, f32[128]{0:T(128)S(1)} %get-tuple-element.323, f32[128,128]{1,0:T(8,128)S(1)} %get-tuple-element.324, f32[128]{0:T(128)S(1)} %broadcast_multiply_fusion.2, ...), kind=kLoop, calls=%fused_computation.7.clone.1 | loop fusion | flops 35651584 | bytes 33753600 | tf_op jit(solution)/shard_map/while/body/eval_jaxpr/sub | solution.py:116
  119.4 12.1 %fusion.188 = (f32[128,128,128]{2,1,0:T(8,128)}, f32[128,128,128]{2,1,0:T(8,128)}) fusion(f32[128,128,128]{2,1,0:T(8,128)} %get-tuple-element.340, f32[128,128]{1,0:T(8,128)S(1)} %get-tuple-element.321, f32[128]{0:T(128)S(1)} %get-tuple-element.323, f32[128,128]{1,0:T(8,128)S(1)} %get-tuple-element.324, f32[128]{0:T(128)S(1)} %broadcast_multiply_fusion.2, ...), kind=kLoop, calls=%fused_computation.7.clone.1 | loop fusion | flops 35651584 | bytes 33753600 | tf_op jit(solution)/shard_map/while/body/eval_jaxpr/sub | solution.py:116
  132.1 12.1 %fusion.188 = (f32[128,128,128]{2,1,0:T(8,128)}, f32[128,128,128]{2,1,0:T(8,128)}) fusion(f32[128,128,128]{2,1,0:T(8,128)} %get-tuple-element.340, f32[128,128]{1,0:T(8,128)S(1)} %get-tuple-element.321, f32[128]{0:T(128)S(1)} %get-tuple-element.323, f32[128,128]{1,0:T(8,128)S(1)} %get-tuple-element.324, f32[128]{0:T(128)S(1)} %broadcast_multiply_fusion.2, ...), kind=kLoop, calls=%fused_computation.7.clone.1 | loop fusion | flops 35651584 | bytes 33753600 | tf_op jit(solution)/shard_map/while/body/eval_jaxpr/sub | solution.py:116
  144.7 12.1 %fusion.188 = (f32[128,128,128]{2,1,0:T(8,128)}, f32[128,128,128]{2,1,0:T(8,128)}) fusion(f32[128,128,128]{2,1,0:T(8,128)} %get-tuple-element.340, f32[128,128]{1,0:T(8,128)S(1)} %get-tuple-element.321, f32[128]{0:T(128)S(1)} %get-tuple-element.323, f32[128,128]{1,0:T(8,128)S(1)} %get-tuple-element.324, f32[128]{0:T(128)S(1)} %broadcast_multiply_fusion.2, ...), kind=kLoop, calls=%fused_computation.7.clone.1 | loop fusion | flops 35651584 | bytes 33753600 | tf_op jit(solution)/shard_map/while/body/eval_jaxpr/sub | solution.py:116
  157.4 12.1 %fusion.188 = (f32[128,128,128]{2,1,0:T(8,128)}, f32[128,128,128]{2,1,0:T(8,128)}) fusion(f32[128,128,128]{2,1,0:T(8,128)} %get-tuple-element.340, f32[128,128]{1,0:T(8,128)S(1)} %get-tuple-element.321, f32[128]{0:T(128)S(1)} %get-tuple-element.323, f32[128,128]{1,0:T(8,128)S(1)} %get-tuple-element.324, f32[128]{0:T(128)S(1)} %broadcast_multiply_fusion.2, ...), kind=kLoop, calls=%fused_computation.7.clone.1 | loop fusion | flops 35651584 | bytes 33753600 | tf_op jit(solution)/shard_map/while/body/eval_jaxpr/sub | solution.py:116
  170.1 12.1 %fusion.188 = (f32[128,128,128]{2,1,0:T(8,128)}, f32[128,128,128]{2,1,0:T(8,128)}) fusion(f32[128,128,128]{2,1,0:T(8,128)} %get-tuple-element.340, f32[128,128]{1,0:T(8,128)S(1)} %get-tuple-element.321, f32[128]{0:T(128)S(1)} %get-tuple-element.323, f32[128,128]{1,0:T(8,128)S(1)} %get-tuple-element.324, f32[128]{0:T(128)S(1)} %broadcast_multiply_fusion.2, ...), kind=kLoop, calls=%fused_computation.7.clone.1 | loop fusion | flops 35651584 | bytes 33753600 | tf_op jit(solution)/shard_map/while/body/eval_jaxpr/sub | solution.py:116
  182.7 12.1 %fusion.188 = (f32[128,128,128]{2,1,0:T(8,128)}, f32[128,128,128]{2,1,0:T(8,128)}) fusion(f32[128,128,128]{2,1,0:T(8,128)} %get-tuple-element.340, f32[128,128]{1,0:T(8,128)S(1)} %get-tuple-element.321, f32[128]{0:T(128)S(1)} %get-tuple-element.323, f32[128,128]{1,0:T(8,128)S(1)} %get-tuple-element.324, f32[128]{0:T(128)S(1)} %broadcast_multiply_fusion.2, ...), kind=kLoop, calls=%fused_computation.7.clone.1 | loop fusion | flops 35651584 | bytes 33753600 | tf_op jit(solution)/shard_map/while/body/eval_jaxpr/sub | solution.py:116
  195.4 12.1 %fusion.188 = (f32[128,128,128]{2,1,0:T(8,128)}, f32[128,128,128]{2,1,0:T(8,128)}) fusion(f32[128,128,128]{2,1,0:T(8,128)} %get-tuple-element.340, f32[128,128]{1,0:T(8,128)S(1)} %get-tuple-element.321, f32[128]{0:T(128)S(1)} %get-tuple-element.323, f32[128,128]{1,0:T(8,128)S(1)} %get-tuple-element.324, f32[128]{0:T(128)S(1)} %broadcast_multiply_fusion.2, ...), kind=kLoop, calls=%fused_computation.7.clone.1 | loop fusion | flops 35651584 | bytes 33753600 | tf_op jit(solution)/shard_map/while/body/eval_jaxpr/sub | solution.py:116
  208.1 12.1 %fusion.188 = (f32[128,128,128]{2,1,0:T(8,128)}, f32[128,128,128]{2,1,0:T(8,128)}) fusion(f32[128,128,128]{2,1,0:T(8,128)} %get-tuple-element.340, f32[128,128]{1,0:T(8,128)S(1)} %get-tuple-element.321, f32[128]{0:T(128)S(1)} %get-tuple-element.323, f32[128,128]{1,0:T(8,128)S(1)} %get-tuple-element.324, f32[128]{0:T(128)S(1)} %broadcast_multiply_fusion.2, ...), kind=kLoop, calls=%fused_computation.7.clone.1 | loop fusion | flops 35651584 | bytes 33753600 | tf_op jit(solution)/shard_map/while/body/eval_jaxpr/sub | solution.py:116
  220.7 12.1 %fusion.188 = (f32[128,128,128]{2,1,0:T(8,128)}, f32[128,128,128]{2,1,0:T(8,128)}) fusion(f32[128,128,128]{2,1,0:T(8,128)} %get-tuple-element.340, f32[128,128]{1,0:T(8,128)S(1)} %get-tuple-element.321, f32[128]{0:T(128)S(1)} %get-tuple-element.323, f32[128,128]{1,0:T(8,128)S(1)} %get-tuple-element.324, f32[128]{0:T(128)S(1)} %broadcast_multiply_fusion.2, ...), kind=kLoop, calls=%fused_computation.7.clone.1 | loop fusion | flops 35651584 | bytes 33753600 | tf_op jit(solution)/shard_map/while/body/eval_jaxpr/sub | solution.py:116
  233.4 12.1 %fusion.188 = (f32[128,128,128]{2,1,0:T(8,128)}, f32[128,128,128]{2,1,0:T(8,128)}) fusion(f32[128,128,128]{2,1,0:T(8,128)} %get-tuple-element.340, f32[128,128]{1,0:T(8,128)S(1)} %get-tuple-element.321, f32[128]{0:T(128)S(1)} %get-tuple-element.323, f32[128,128]{1,0:T(8,128)S(1)} %get-tuple-element.324, f32[128]{0:T(128)S(1)} %broadcast_multiply_fusion.2, ...), kind=kLoop, calls=%fused_computation.7.clone.1 | loop fusion | flops 35651584 | bytes 33753600 | tf_op jit(solution)/shard_map/while/body/eval_jaxpr/sub | solution.py:116
  246.1 12.1 %fusion.188 = (f32[128,128,128]{2,1,0:T(8,128)}, f32[128,128,128]{2,1,0:T(8,128)}) fusion(f32[128,128,128]{2,1,0:T(8,128)} %get-tuple-element.340, f32[128,128]{1,0:T(8,128)S(1)} %get-tuple-element.321, f32[128]{0:T(128)S(1)} %get-tuple-element.323, f32[128,128]{1,0:T(8,128)S(1)} %get-tuple-element.324, f32[128]{0:T(128)S(1)} %broadcast_multiply_fusion.2, ...), kind=kLoop, calls=%fused_computation.7.clone.1 | loop fusion | flops 35651584 | bytes 33753600 | tf_op jit(solution)/shard_map/while/body/eval_jaxpr/sub | solution.py:116
  258.7 12.1 %fusion.188 = (f32[128,128,128]{2,1,0:T(8,128)}, f32[128,128,128]{2,1,0:T(8,128)}) fusion(f32[128,128,128]{2,1,0:T(8,128)} %get-tuple-element.340, f32[128,128]{1,0:T(8,128)S(1)} %get-tuple-element.321, f32[128]{0:T(128)S(1)} %get-tuple-element.323, f32[128,128]{1,0:T(8,128)S(1)} %get-tuple-element.324, f32[128]{0:T(128)S(1)} %broadcast_multiply_fusion.2, ...), kind=kLoop, calls=%fused_computation.7.clone.1 | loop fusion | flops 35651584 | bytes 33753600 | tf_op jit(solution)/shard_map/while/body/eval_jaxpr/sub | solution.py:116
  287.9 11.7 %multiply_add_fusion.1 = (f32[128,128,128]{2,0,1:T(8,128)S(1)}, f32[128,128,128]{2,0,1:T(8,128)S(1)}) fusion(f32[128,128]{0,1:T(8,128)S(1)} %copy.72, f32[128,128]{0,1:T(8,128)S(1)} %copy.69, f32[128,128,128]{2,0,1:T(8,128)S(1)} %fusion.58, f32[128,128,128]{2,0,1:T(8,128)} %fusion.56, f32[128,128,128]{2,0,1:T(8,128)} %fusion.54, ...), kind=kOutput, calls=%fused_computation.52 | convolution fusion | flops 287457280 | bytes 44171264 | tf_op jit(solution)/shard_map/ka,abc->kbc/dot_general | solution.py:59
  299.6 17.5 %fusion.31 = f32[128,128,128]{2,0,1:T(8,128)} fusion(f32[128,128,128]{2,0,1:T(8,128)S(1)} %get-tuple-element.264), kind=kOutput, calls=%fused_computation.58 | convolution fusion | flops 3221454848 | bytes 16777216 | tf_op jit(solution)/shard_map/kbc,bm->kmc/dot_general | solution.py:37
  317.1 17.6 %fusion.33 = f32[128,128,128]{2,0,1:T(8,128)} fusion(f32[128,128,128]{2,0,1:T(8,128)S(1)} %get-tuple-element.264), kind=kOutput, calls=%fused_computation.60 | convolution fusion | flops 3221454848 | bytes 16777216 | tf_op jit(solution)/shard_map/kbc,bm->kmc/dot_general | solution.py:37
  334.7 17.7 %fusion.29 = f32[128,128,128]{2,0,1:T(8,128)} fusion(f32[128,128,128]{2,0,1:T(8,128)S(1)} %get-tuple-element.265), kind=kOutput, calls=%fused_computation.56 | convolution fusion | flops 3221454848 | bytes 16777216 | tf_op jit(solution)/shard_map/kbc,bm->kmc/dot_general | solution.py:37
  352.4 27.7 %fusion.25 = (f32[128,128,128]{2,1,0:T(8,128)}, f32[128,128,128]{2,1,0:T(8,128)}) fusion(f32[128,128,128]{2,1,0:T(8,128)} %get-tuple-element.149, f32[128,128,128]{2,1,0:T(8,128)} %get-tuple-element.148, f32[128,128,128]{2,0,1:T(8,128)} %fusion.31, f32[128,128,128]{2,0,1:T(8,128)} %fusion.33, f32[128,128,128]{2,0,1:T(8,128)} %fusion.29, ...), kind=kOutput, calls=%fused_computation.45 | convolution fusion | flops 3238232064 | bytes 67108864 | tf_op jit(solution)/shard_map/kbc,bm->kmc/dot_general | solution.py:37
  380.2 11.7 %fusion.74 = f32[128,128,128]{2,0,1:T(8,128)S(1)} fusion(f32[128,128,128]{2,1,0:T(8,128)} %get-tuple-element.262), kind=kOutput, calls=%fused_computation.118 | convolution fusion | flops 3221454848 | bytes 16777216 | tf_op jit(solution)/shard_map/kmc,bm->kbc/dot_general | solution.py:37
  400.5 10.9 %fusion.66 = f32[128,128,128]{2,0,1:T(8,128)S(1)} fusion(f32[128,128,128]{2,1,0:T(8,128)} %get-tuple-element.263), kind=kOutput, calls=%fused_computation.110 | convolution fusion | flops 3221454848 | bytes 16777216 | tf_op jit(solution)/shard_map/kmc,bm->kbc/dot_general | solution.py:37
  411.4 12.1 %fusion.72 = f32[128,128,128]{2,0,1:T(8,128)} fusion(f32[128,128,128]{2,1,0:T(8,128)} %get-tuple-element.263), kind=kOutput, calls=%fused_computation.116 | convolution fusion | flops 3221454848 | bytes 16777216 | tf_op jit(solution)/shard_map/kmc,bm->kbc/dot_general | solution.py:37
  423.5 33.1 %fusion.20 = f32[64,128,128]{2,0,1:T(8,128)} fusion(f32[128,128]{0,1:T(8,128)S(1)} %copy.72, f32[128,128]{0,1:T(8,128)S(1)} %copy.69, f32[128,128,128]{2,0,1:T(8,128)S(1)} %fusion.66, f32[128,128,128]{2,0,1:T(8,128)S(1)} %fusion.74, f32[128,128,128]{2,0,1:T(8,128)S(1)} %fusion.64, f32[128,128,128]{2,0,1:T(8,128)} %fusion.72), kind=kOutput, calls=%fused_computation.38 | convolution fusion | flops 1621213184 | bytes 37879808 | tf_op jit(solution)/shard_map/ka,kbc->abc/dot_general | solution.py:37
  456.6 33.1 %subtract_multiply_fusion = f32[64,128,128]{2,0,1:T(8,128)} fusion(f32[64,128,128]{2,0,1:T(8,128)} %fusion.20, f32[128,128]{0,1:T(8,128)S(1)} %copy.72, f32[128,128]{0,1:T(8,128)S(1)} %copy.69, f32[128,128,128]{2,0,1:T(8,128)S(1)} %fusion.66, f32[128,128,128]{2,0,1:T(8,128)S(1)} %fusion.74, f32[128,128,128]{2,0,1:T(8,128)S(1)} %fusion.64, ...), kind=kOutput, calls=%fused_computation.86 | convolution fusion | flops 1623310336 | bytes 42074112 | tf_op jit(solution)/shard_map/ka,kbc->abc/dot_general | solution.py:37
  503.7 53.0 %all-to-all-done.1 = f32[16,512,128]{2,1,0:T(8,128)} async-done(((f32[16,512,128]{2,1,0:T(8,128)}), f32[16,512,128]{2,1,0:T(8,128)}, u32[]{:S(2)}, u32[]{:S(2)}) %all-to-all-start.1) | async-done | bytes 4194336 | tf_op jit(solution)/shard_map/all_to_all | solution.py:167
  569.4 13.9 %convolution_convert_fusion = bf16[512,4096]{1,0:T(8,128)(2,1)} fusion(bf16[512,2048]{0,1:T(8,128)(2,1)S(1)} %fusion.45, bf16[2048,4096]{1,0:T(8,128)(2,1)} %param.15), kind=kOutput, calls=%fused_computation.69 | convolution fusion | flops 8592031744 | bytes 23068672 | tf_op jit(solution)/shard_map/dot_general | solution.py:171
  583.3 64.9 %reduce-scatter.2.cloned.1.call-done = bf16[256,4096]{1,0:T(8,128)(2,1)} async-done(((bf16[512,4096]{1,0:T(8,128)(2,1)}), bf16[256,4096]{1,0:T(8,128)(2,1)}) %reduce-scatter.2.cloned.1.call-update) | async-done | bytes 2097168 | tf_op jit(solution)/shard_map/reduce_scatter | solution.py:170
  (129 shorter events, 95.4 us)
Async XLA Ops:
  7.5 20.1 %collective-permute-start = (bf16[2,3,2048]{2,0,1:T(2,128)(2,1)S(1)}, bf16[2,3,2048]{2,0,1:T(2,128)(2,1)S(1)}, u32[]{:S(2)}, u32[]{:S(2)}) collective-permute-start(bf16[2,3,2048]{2,0,1:T(2,128)(2,1)S(1)} %slice.37), channel_id=1, source_target_pairs={{0,8},{8,16},{16,24},{24,32},{32,40},{40,48},{48,56},{56,64},{64,7... | collective-permute-start | bytes 73736 | tf_op jit(solution)/shard_map/ppermute | solution.py:15
  18.2 44.9 %copy-start.4 = (s32[512]{0:T(512)}, s32[512]{0:T(512)S(1)}, u32[]{:S(2)}) copy-start(s32[512]{0:T(512)S(1)} %multiply_add_fusion.2) | copy-start | bytes 6148
  57.4 4.5 copy-start
  66.0 205.5 %all-to-all-start = ((bf16[512,16,128]{0,2,1:T(8,128)(2,1)}), bf16[512,16,128]{0,2,1:T(8,128)(2,1)S(1)}, u32[]{:S(2)}, u32[]{:S(2)}) async-start(bf16[512,16,128]{0,2,1:T(8,128)(2,1)} %select_convert_fusion), calls=%async_computation | async-start | bytes 4194304 | tf_op jit(solution)/shard_map/all_to_all | solution.py:163
  271.5 1.3 copy-start.3
  299.6 35.1 %copy-start.2 = (f32[128,128,128]{2,0,1:T(8,128)}, f32[128,128,128]{2,0,1:T(8,128)S(1)}, u32[]{:S(2)}) copy-start(f32[128,128,128]{2,0,1:T(8,128)S(1)} %get-tuple-element.265) | copy-start | bytes 25165828
  380.2 11.7 %copy-start.1 = (f32[128,128,128]{2,1,0:T(8,128)S(1)}, f32[128,128,128]{2,1,0:T(8,128)}, u32[]{:S(2)}) copy-start(f32[128,128,128]{2,1,0:T(8,128)} %get-tuple-element.262) | copy-start | bytes 25165828
  496.2 66.0 %copy-start.5 = (s32[512]{0:T(512)S(1)}, s32[512]{0:T(512)}, u32[]{:S(2)}) copy-start(s32[512]{0:T(512)} %copy-done.4) | copy-start | bytes 6148
  496.3 66.0 %copy-start.6 = (f32[2048]{0:T(1024)S(1)}, f32[2048]{0:T(1024)}, u32[]{:S(2)}) copy-start(f32[2048]{0:T(1024)} %param.13) | copy-start | bytes 24580
  496.3 60.5 %all-to-all-start.1 = ((f32[16,512,128]{2,1,0:T(8,128)}), f32[16,512,128]{2,1,0:T(8,128)}, u32[]{:S(2)}, u32[]{:S(2)}) async-start(f32[16,512,128]{2,1,0:T(8,128)} %bitcast.146), calls=%async_computation.1 | async-start | bytes 8388608 | tf_op jit(solution)/shard_map/all_to_all | solution.py:167
  503.6 144.6 %reduce-scatter.2.cloned.1.call-start = ((), (), s32[]{:S(2)}) async-start(), calls=%async_computation.3 | async-start | bytes 6291456 | tf_op jit(solution)/shard_map/reduce_scatter | solution.py:170
Sparse Core Ops, SparseCore 0:
  583.5 64.7 reduce-scatter.1
where the time goes:
time: 663 us; the launch traced here: 655 us
  other arithmetic  241 us (36%)
  matrix products  228 us (34%)
  waiting for transfers between devices  118 us (18%)
  local copies, waits for them, and re-layouts  34.1 us (5%)
  starting transfers between devices  19.1 us (3%)
  between operations  14.5 us (2%)
    sub x16, other arithmetic, add_mode(): return (totals[0] + scale * denom_real, totals[1] - scale * denom_imag)  191 us
    dot_general x10, matrix products, contract(): return jnp.einsum(form, left, right, precision=precise)  190 us
    reduce_scatter x1, waiting for transfers between devices, body(): lax.psum_scatter(jnp.dot(mixed, out_weight, preferred_element_type=jnp.fl...  64.9 us
    all_to_all x1, waiting for transfers between devices, body(): lax.all_to_all(convolved, 'ctx', split_axis=0, concat_axis=1, tiled=True)  53 us
    add x1, other arithmetic, body(): filtered + short_filter[:, lag, :][None] * joined[SHORT - 1 - lag:SHORT -...  17.3 us
    dot_general x2, matrix products, narrow_section(): jnp.einsum('ka,abc->kbc', lower, grid, preferred_element_type=jnp.float32)  16.9 us
    unnamed x17, local copies, waits for them, and re-layouts  14.5 us
    dot_general x1, matrix products, body(): jnp.dot(mixed, out_weight, preferred_element_type=jnp.float32)  13.9 us
  transfers between devices with their start and end apart: 4, of which 2 were waited for; matrix products, arithmetic and copies ran while one was open for 32% of the time, Pallas kernels for 0%

commit v1 on v0

--- a/solution.py
+++ b/solution.py
@@ -164,7 +164,10 @@
     residue_part = lax.dynamic_slice_in_dim(mode_residue, ctx_index * col_width, col_width, 1)
     mix_part = lax.dynamic_slice_in_dim(decay_mix, ctx_index * col_width, col_width, 1)
     convolved = causal_fft(columns, residue_part, mix_part)
-    conv_out = lax.all_to_all(convolved, "ctx", split_axis=0, concat_axis=1, tiled=True)
+    peers = lax.axis_size("ctx")
+    blocks = jnp.stack(jnp.split(convolved, peers, axis=0), axis=0)
+    blocks = lax.all_to_all(blocks, "ctx", split_axis=0, concat_axis=0)
+    conv_out = jnp.concatenate(blocks, axis=1)
     long_out = conv_out + skip_gain[None, :] * gated_wide
     mixed = (query * long_out).astype(jnp.bfloat16)
     return lax.psum_scatter(

time: 663 us -> 673 us (1.015)
  local copies, waits for them, and re-layouts: 34.1 us -> 43.7 us
    unnamed x17 -> x32, local copies, waits for them, and re-layouts: 14.5 us -> 25.3 us
where the time goes in v1:
time: 673 us; the launch traced here: 665 us
  other arithmetic  241 us (36%)
  matrix products  228 us (34%)
  waiting for transfers between devices  118 us (18%)
  local copies, waits for them, and re-layouts  43.7 us (6%)
  starting transfers between devices  19.1 us (3%)
  between operations  14.6 us (2%)
    sub x16, other arithmetic, add_mode(): return (totals[0] + scale * denom_real, totals[1] - scale * denom_imag)  191 us
    dot_general x10, matrix products, contract(): return jnp.einsum(form, left, right, precision=precise)  190 us
    reduce_scatter x1, waiting for transfers between devices, body(): lax.psum_scatter(jnp.dot(mixed, out_weight, preferred_element_type=jnp.fl...  64.9 us
    all_to_all x1, waiting for transfers between devices, body(): blocks = lax.all_to_all(blocks, 'ctx', split_axis=0, concat_axis=0)  53 us
    unnamed x32, local copies, waits for them, and re-layouts  25.3 us
    add x1, other arithmetic, body(): filtered + short_filter[:, lag, :][None] * joined[SHORT - 1 - lag:SHORT -...  17.3 us
    dot_general x2, matrix products, narrow_section(): jnp.einsum('ka,abc->kbc', lower, grid, preferred_element_type=jnp.float32)  16.9 us
    dot_general x1, matrix products, body(): jnp.dot(mixed, out_weight, preferred_element_type=jnp.float32)  14 us
  transfers between devices with their start and end apart: 4, of which 2 were waited for; matrix products, arithmetic and copies ran while one was open for 32% of the time, Pallas kernels for 0%

profile of v1, /device:TPU:1, one launch (start us, length us, event | category | flops | bytes accessed | tf_op | source)
XLA Modules:
  0.0 665.0 jit_solution(1874849245776220313)
XLA Ops:
  28.4 11.6 %maximum_convert_fusion = f32[514,3,2048]{0,2,1:T(8,128)} fusion(bf16[512,3,2048]{0,2,1:T(8,128)(2,1)} %copy.95, bf16[2,3,2048]{0,2,1:T(8,128)(2,1)S(1)} %copy.94), kind=kLoop, calls=%fused_computation.62 | loop fusion | flops 12632064 | bytes 18948096 | tf_op jit(solution)/shard_map/convert_element_type | solution.py:146
  40.0 17.3 %fusion.17 = f32[512,3,2048]{0,2,1:T(8,128)S(1)} fusion(f32[514,3,2048]{0,2,1:T(8,128)} %maximum_convert_fusion, f32[3,2048]{1,0:T(4,128)S(1)} %get-tuple-element.287, f32[3,2048]{1,0:T(4,128)S(1)} %get-tuple-element.288, f32[3,2048]{1,0:T(4,128)S(1)} %bitcast.211), kind=kLoop, calls=%fused_computation.31 | loop fusion | flops 15728640 | bytes 50405376 | tf_op jit(solution)/shard_map/add | solution.py:150
  70.8 199.8 %while.19 = (s32[]{:T(128)}, f32[128,128,128]{2,1,0:T(8,128)}, f32[128,128,128]{2,1,0:T(8,128)}, f32[16,128]{1,0:T(8,128)S(1)}, f32[16,128]{1,0:T(8,128)S(1)}, /*index=5*/s32[128]{0:T(128)S(1)}, s32[]{:T(128)}, s32[]{:T(128)}) while((s32[]{:T(128)}, f32[128,128,128]{2,1,0:T(8,128)}, ...), condition=%wide.region_1.2_spmd.clone.clone.clone.clone, body=%wide.region_0.1_spmd.clone.clone.clone.clone.sunk | while | flops 35963392 | bytes 33956460 | solution.py:119
  71.3 9.4 %fusion.189 = (f32[128,128,128]{2,1,0:T(8,128)}, f32[128,128,128]{2,1,0:T(8,128)}) fusion(f32[128,128,128]{2,1,0:T(8,128)} %get-tuple-element.356, f32[128,128]{1,0:T(8,128)S(1)} %get-tuple-element.337, f32[128]{0:T(128)S(1)} %get-tuple-element.339, f32[128,128]{1,0:T(8,128)S(1)} %get-tuple-element.340, f32[128]{0:T(128)S(1)} %broadcast_multiply_fusion.2, ...), kind=kLoop, calls=%fused_computation.7.clone.1 | loop fusion | flops 35651584 | bytes 33753600 | tf_op jit(solution)/shard_map/while/body/eval_jaxpr/sub | solution.py:116
  81.3 12.1 %fusion.189 = (f32[128,128,128]{2,1,0:T(8,128)}, f32[128,128,128]{2,1,0:T(8,128)}) fusion(f32[128,128,128]{2,1,0:T(8,128)} %get-tuple-element.356, f32[128,128]{1,0:T(8,128)S(1)} %get-tuple-element.337, f32[128]{0:T(128)S(1)} %get-tuple-element.339, f32[128,128]{1,0:T(8,128)S(1)} %get-tuple-element.340, f32[128]{0:T(128)S(1)} %broadcast_multiply_fusion.2, ...), kind=kLoop, calls=%fused_computation.7.clone.1 | loop fusion | flops 35651584 | bytes 33753600 | tf_op jit(solution)/shard_map/while/body/eval_jaxpr/sub | solution.py:116
  94.0 12.1 %fusion.189 = (f32[128,128,128]{2,1,0:T(8,128)}, f32[128,128,128]{2,1,0:T(8,128)}) fusion(f32[128,128,128]{2,1,0:T(8,128)} %get-tuple-element.356, f32[128,128]{1,0:T(8,128)S(1)} %get-tuple-element.337, f32[128]{0:T(128)S(1)} %get-tuple-element.339, f32[128,128]{1,0:T(8,128)S(1)} %get-tuple-element.340, f32[128]{0:T(128)S(1)} %broadcast_multiply_fusion.2, ...), kind=kLoop, calls=%fused_computation.7.clone.1 | loop fusion | flops 35651584 | bytes 33753600 | tf_op jit(solution)/shard_map/while/body/eval_jaxpr/sub | solution.py:116
  106.6 12.1 %fusion.189 = (f32[128,128,128]{2,1,0:T(8,128)}, f32[128,128,128]{2,1,0:T(8,128)}) fusion(f32[128,128,128]{2,1,0:T(8,128)} %get-tuple-element.356, f32[128,128]{1,0:T(8,128)S(1)} %get-tuple-element.337, f32[128]{0:T(128)S(1)} %get-tuple-element.339, f32[128,128]{1,0:T(8,128)S(1)} %get-tuple-element.340, f32[128]{0:T(128)S(1)} %broadcast_multiply_fusion.2, ...), kind=kLoop, calls=%fused_computation.7.clone.1 | loop fusion | flops 35651584 | bytes 33753600 | tf_op jit(solution)/shard_map/while/body/eval_jaxpr/sub | solution.py:116
  119.3 12.1 %fusion.189 = (f32[128,128,128]{2,1,0:T(8,128)}, f32[128,128,128]{2,1,0:T(8,128)}) fusion(f32[128,128,128]{2,1,0:T(8,128)} %get-tuple-element.356, f32[128,128]{1,0:T(8,128)S(1)} %get-tuple-element.337, f32[128]{0:T(128)S(1)} %get-tuple-element.339, f32[128,128]{1,0:T(8,128)S(1)} %get-tuple-element.340, f32[128]{0:T(128)S(1)} %broadcast_multiply_fusion.2, ...), kind=kLoop, calls=%fused_computation.7.clone.1 | loop fusion | flops 35651584 | bytes 33753600 | tf_op jit(solution)/shard_map/while/body/eval_jaxpr/sub | solution.py:116
  131.9 12.1 %fusion.189 = (f32[128,128,128]{2,1,0:T(8,128)}, f32[128,128,128]{2,1,0:T(8,128)}) fusion(f32[128,128,128]{2,1,0:T(8,128)} %get-tuple-element.356, f32[128,128]{1,0:T(8,128)S(1)} %get-tuple-element.337, f32[128]{0:T(128)S(1)} %get-tuple-element.339, f32[128,128]{1,0:T(8,128)S(1)} %get-tuple-element.340, f32[128]{0:T(128)S(1)} %broadcast_multiply_fusion.2, ...), kind=kLoop, calls=%fused_computation.7.clone.1 | loop fusion | flops 35651584 | bytes 33753600 | tf_op jit(solution)/shard_map/while/body/eval_jaxpr/sub | solution.py:116
  144.6 12.1 %fusion.189 = (f32[128,128,128]{2,1,0:T(8,128)}, f32[128,128,128]{2,1,0:T(8,128)}) fusion(f32[128,128,128]{2,1,0:T(8,128)} %get-tuple-element.356, f32[128,128]{1,0:T(8,128)S(1)} %get-tuple-element.337, f32[128]{0:T(128)S(1)} %get-tuple-element.339, f32[128,128]{1,0:T(8,128)S(1)} %get-tuple-element.340, f32[128]{0:T(128)S(1)} %broadcast_multiply_fusion.2, ...), kind=kLoop, calls=%fused_computation.7.clone.1 | loop fusion | flops 35651584 | bytes 33753600 | tf_op jit(solution)/shard_map/while/body/eval_jaxpr/sub | solution.py:116
  157.3 12.1 %fusion.189 = (f32[128,128,128]{2,1,0:T(8,128)}, f32[128,128,128]{2,1,0:T(8,128)}) fusion(f32[128,128,128]{2,1,0:T(8,128)} %get-tuple-element.356, f32[128,128]{1,0:T(8,128)S(1)} %get-tuple-element.337, f32[128]{0:T(128)S(1)} %get-tuple-element.339, f32[128,128]{1,0:T(8,128)S(1)} %get-tuple-element.340, f32[128]{0:T(128)S(1)} %broadcast_multiply_fusion.2, ...), kind=kLoop, calls=%fused_computation.7.clone.1 | loop fusion | flops 35651584 | bytes 33753600 | tf_op jit(solution)/shard_map/while/body/eval_jaxpr/sub | solution.py:116
  169.9 12.1 %fusion.189 = (f32[128,128,128]{2,1,0:T(8,128)}, f32[128,128,128]{2,1,0:T(8,128)}) fusion(f32[128,128,128]{2,1,0:T(8,128)} %get-tuple-element.356, f32[128,128]{1,0:T(8,128)S(1)} %get-tuple-element.337, f32[128]{0:T(128)S(1)} %get-tuple-element.339, f32[128,128]{1,0:T(8,128)S(1)} %get-tuple-element.340, f32[128]{0:T(128)S(1)} %broadcast_multiply_fusion.2, ...), kind=kLoop, calls=%fused_computation.7.clone.1 | loop fusion | flops 35651584 | bytes 33753600 | tf_op jit(solution)/shard_map/while/body/eval_jaxpr/sub | solution.py:116
  182.6 12.1 %fusion.189 = (f32[128,128,128]{2,1,0:T(8,128)}, f32[128,128,128]{2,1,0:T(8,128)}) fusion(f32[128,128,128]{2,1,0:T(8,128)} %get-tuple-element.356, f32[128,128]{1,0:T(8,128)S(1)} %get-tuple-element.337, f32[128]{0:T(128)S(1)} %get-tuple-element.339, f32[128,128]{1,0:T(8,128)S(1)} %get-tuple-element.340, f32[128]{0:T(128)S(1)} %broadcast_multiply_fusion.2, ...), kind=kLoop, calls=%fused_computation.7.clone.1 | loop fusion | flops 35651584 | bytes 33753600 | tf_op jit(solution)/shard_map/while/body/eval_jaxpr/sub | solution.py:116
  195.2 12.1 %fusion.189 = (f32[128,128,128]{2,1,0:T(8,128)}, f32[128,128,128]{2,1,0:T(8,128)}) fusion(f32[128,128,128]{2,1,0:T(8,128)} %get-tuple-element.356, f32[128,128]{1,0:T(8,128)S(1)} %get-tuple-element.337, f32[128]{0:T(128)S(1)} %get-tuple-element.339, f32[128,128]{1,0:T(8,128)S(1)} %get-tuple-element.340, f32[128]{0:T(128)S(1)} %broadcast_multiply_fusion.2, ...), kind=kLoop, calls=%fused_computation.7.clone.1 | loop fusion | flops 35651584 | bytes 33753600 | tf_op jit(solution)/shard_map/while/body/eval_jaxpr/sub | solution.py:116
  207.9 12.1 %fusion.189 = (f32[128,128,128]{2,1,0:T(8,128)}, f32[128,128,128]{2,1,0:T(8,128)}) fusion(f32[128,128,128]{2,1,0:T(8,128)} %get-tuple-element.356, f32[128,128]{1,0:T(8,128)S(1)} %get-tuple-element.337, f32[128]{0:T(128)S(1)} %get-tuple-element.339, f32[128,128]{1,0:T(8,128)S(1)} %get-tuple-element.340, f32[128]{0:T(128)S(1)} %broadcast_multiply_fusion.2, ...), kind=kLoop, calls=%fused_computation.7.clone.1 | loop fusion | flops 35651584 | bytes 33753600 | tf_op jit(solution)/shard_map/while/body/eval_jaxpr/sub | solution.py:116
  220.5 12.1 %fusion.189 = (f32[128,128,128]{2,1,0:T(8,128)}, f32[128,128,128]{2,1,0:T(8,128)}) fusion(f32[128,128,128]{2,1,0:T(8,128)} %get-tuple-element.356, f32[128,128]{1,0:T(8,128)S(1)} %get-tuple-element.337, f32[128]{0:T(128)S(1)} %get-tuple-element.339, f32[128,128]{1,0:T(8,128)S(1)} %get-tuple-element.340, f32[128]{0:T(128)S(1)} %broadcast_multiply_fusion.2, ...), kind=kLoop, calls=%fused_computation.7.clone.1 | loop fusion | flops 35651584 | bytes 33753600 | tf_op jit(solution)/shard_map/while/body/eval_jaxpr/sub | solution.py:116
  233.2 12.1 %fusion.189 = (f32[128,128,128]{2,1,0:T(8,128)}, f32[128,128,128]{2,1,0:T(8,128)}) fusion(f32[128,128,128]{2,1,0:T(8,128)} %get-tuple-element.356, f32[128,128]{1,0:T(8,128)S(1)} %get-tuple-element.337, f32[128]{0:T(128)S(1)} %get-tuple-element.339, f32[128,128]{1,0:T(8,128)S(1)} %get-tuple-element.340, f32[128]{0:T(128)S(1)} %broadcast_multiply_fusion.2, ...), kind=kLoop, calls=%fused_computation.7.clone.1 | loop fusion | flops 35651584 | bytes 33753600 | tf_op jit(solution)/shard_map/while/body/eval_jaxpr/sub | solution.py:116
  245.9 12.1 %fusion.189 = (f32[128,128,128]{2,1,0:T(8,128)}, f32[128,128,128]{2,1,0:T(8,128)}) fusion(f32[128,128,128]{2,1,0:T(8,128)} %get-tuple-element.356, f32[128,128]{1,0:T(8,128)S(1)} %get-tuple-element.337, f32[128]{0:T(128)S(1)} %get-tuple-element.339, f32[128,128]{1,0:T(8,128)S(1)} %get-tuple-element.340, f32[128]{0:T(128)S(1)} %broadcast_multiply_fusion.2, ...), kind=kLoop, calls=%fused_computation.7.clone.1 | loop fusion | flops 35651584 | bytes 33753600 | tf_op jit(solution)/shard_map/while/body/eval_jaxpr/sub | solution.py:116
  258.5 12.1 %fusion.189 = (f32[128,128,128]{2,1,0:T(8,128)}, f32[128,128,128]{2,1,0:T(8,128)}) fusion(f32[128,128,128]{2,1,0:T(8,128)} %get-tuple-element.356, f32[128,128]{1,0:T(8,128)S(1)} %get-tuple-element.337, f32[128]{0:T(128)S(1)} %get-tuple-element.339, f32[128,128]{1,0:T(8,128)S(1)} %get-tuple-element.340, f32[128]{0:T(128)S(1)} %broadcast_multiply_fusion.2, ...), kind=kLoop, calls=%fused_computation.7.clone.1 | loop fusion | flops 35651584 | bytes 33753600 | tf_op jit(solution)/shard_map/while/body/eval_jaxpr/sub | solution.py:116
  287.7 11.7 %multiply_add_fusion.1 = (f32[128,128,128]{2,0,1:T(8,128)S(1)}, f32[128,128,128]{2,0,1:T(8,128)S(1)}) fusion(f32[128,128]{0,1:T(8,128)S(1)} %copy.102, f32[128,128]{0,1:T(8,128)S(1)} %copy.99, f32[128,128,128]{2,0,1:T(8,128)S(1)} %fusion.58, f32[128,128,128]{2,0,1:T(8,128)} %fusion.56, f32[128,128,128]{2,0,1:T(8,128)} %fusion.54, ...), kind=kOutput, calls=%fused_computation.52 | convolution fusion | flops 287457280 | bytes 44171264 | tf_op jit(solution)/shard_map/ka,abc->kbc/dot_general | solution.py:59
  299.4 17.5 %fusion.31 = f32[128,128,128]{2,0,1:T(8,128)} fusion(f32[128,128,128]{2,0,1:T(8,128)S(1)} %get-tuple-element.264), kind=kOutput, calls=%fused_computation.58 | convolution fusion | flops 3221454848 | bytes 16777216 | tf_op jit(solution)/shard_map/kbc,bm->kmc/dot_general | solution.py:37
  316.9 17.6 %fusion.33 = f32[128,128,128]{2,0,1:T(8,128)} fusion(f32[128,128,128]{2,0,1:T(8,128)S(1)} %get-tuple-element.264), kind=kOutput, calls=%fused_computation.60 | convolution fusion | flops 3221454848 | bytes 16777216 | tf_op jit(solution)/shard_map/kbc,bm->kmc/dot_general | solution.py:37
  334.5 17.7 %fusion.29 = f32[128,128,128]{2,0,1:T(8,128)} fusion(f32[128,128,128]{2,0,1:T(8,128)S(1)} %get-tuple-element.265), kind=kOutput, calls=%fused_computation.56 | convolution fusion | flops 3221454848 | bytes 16777216 | tf_op jit(solution)/shard_map/kbc,bm->kmc/dot_general | solution.py:37
  352.3 27.7 %fusion.25 = (f32[128,128,128]{2,1,0:T(8,128)}, f32[128,128,128]{2,1,0:T(8,128)}) fusion(f32[128,128,128]{2,1,0:T(8,128)} %get-tuple-element.149, f32[128,128,128]{2,1,0:T(8,128)} %get-tuple-element.148, f32[128,128,128]{2,0,1:T(8,128)} %fusion.31, f32[128,128,128]{2,0,1:T(8,128)} %fusion.33, f32[128,128,128]{2,0,1:T(8,128)} %fusion.29, ...), kind=kOutput, calls=%fused_computation.45 | convolution fusion | flops 3238232064 | bytes 67108864 | tf_op jit(solution)/shard_map/kbc,bm->kmc/dot_general | solution.py:37
  380.0 11.7 %fusion.74 = f32[128,128,128]{2,0,1:T(8,128)S(1)} fusion(f32[128,128,128]{2,1,0:T(8,128)} %get-tuple-element.262), kind=kOutput, calls=%fused_computation.134 | convolution fusion | flops 3221454848 | bytes 16777216 | tf_op jit(solution)/shard_map/kmc,bm->kbc/dot_general | solution.py:37
  400.3 10.9 %fusion.66 = f32[128,128,128]{2,0,1:T(8,128)S(1)} fusion(f32[128,128,128]{2,1,0:T(8,128)} %get-tuple-element.263), kind=kOutput, calls=%fused_computation.126 | convolution fusion | flops 3221454848 | bytes 16777216 | tf_op jit(solution)/shard_map/kmc,bm->kbc/dot_general | solution.py:37
  411.2 12.1 %fusion.72 = f32[128,128,128]{2,0,1:T(8,128)} fusion(f32[128,128,128]{2,1,0:T(8,128)} %get-tuple-element.263), kind=kOutput, calls=%fused_computation.132 | convolution fusion | flops 3221454848 | bytes 16777216 | tf_op jit(solution)/shard_map/kmc,bm->kbc/dot_general | solution.py:37
  423.3 33.1 %fusion.20 = f32[64,128,128]{2,0,1:T(8,128)} fusion(f32[128,128]{0,1:T(8,128)S(1)} %copy.102, f32[128,128]{0,1:T(8,128)S(1)} %copy.99, f32[128,128,128]{2,0,1:T(8,128)S(1)} %fusion.66, f32[128,128,128]{2,0,1:T(8,128)S(1)} %fusion.74, f32[128,128,128]{2,0,1:T(8,128)S(1)} %fusion.64, f32[128,128,128]{2,0,1:T(8,128)} %fusion.72), kind=kOutput, calls=%fused_computation.38 | convolution fusion | flops 1621213184 | bytes 37879808 | tf_op jit(solution)/shard_map/ka,kbc->abc/dot_general | solution.py:37
  456.4 33.1 %subtract_multiply_fusion = f32[64,128,128]{2,0,1:T(8,128)} fusion(f32[64,128,128]{2,0,1:T(8,128)} %fusion.20, f32[128,128]{0,1:T(8,128)S(1)} %copy.102, f32[128,128]{0,1:T(8,128)S(1)} %copy.99, f32[128,128,128]{2,0,1:T(8,128)S(1)} %fusion.66, f32[128,128,128]{2,0,1:T(8,128)S(1)} %fusion.74, f32[128,128,128]{2,0,1:T(8,128)S(1)} %fusion.64, ...), kind=kOutput, calls=%fused_computation.86 | convolution fusion | flops 1623310336 | bytes 42074112 | tf_op jit(solution)/shard_map/ka,kbc->abc/dot_general | solution.py:37
  513.2 53.0 %all-to-all-done.1 = f32[16,512,128]{2,1,0:T(8,128)} async-done(((f32[16,512,128]{2,1,0:T(8,128)}), f32[16,512,128]{2,1,0:T(8,128)}, u32[]{:S(2)}, u32[]{:S(2)}) %all-to-all-start.1) | async-done | bytes 4194336 | tf_op jit(solution)/shard_map/all_to_all | solution.py:169
  579.0 14.0 %convolution_convert_fusion = bf16[512,4096]{1,0:T(8,128)(2,1)} fusion(bf16[512,2048]{0,1:T(8,128)(2,1)S(1)} %fusion.45, bf16[2048,4096]{1,0:T(8,128)(2,1)} %param.15), kind=kOutput, calls=%fused_computation.69 | convolution fusion | flops 8592031744 | bytes 23068672 | tf_op jit(solution)/shard_map/dot_general | solution.py:174
  593.0 64.9 %reduce-scatter.2.cloned.1.call-done = bf16[256,4096]{1,0:T(8,128)(2,1)} async-done(((bf16[512,4096]{1,0:T(8,128)(2,1)}), bf16[256,4096]{1,0:T(8,128)(2,1)}) %reduce-scatter.2.cloned.1.call-update) | async-done | bytes 2097168 | tf_op jit(solution)/shard_map/reduce_scatter | solution.py:173
  (161 shorter events, 104.9 us)
Async XLA Ops:
  7.5 20.0 %collective-permute-start = (bf16[2,3,2048]{2,0,1:T(2,128)(2,1)S(1)}, bf16[2,3,2048]{2,0,1:T(2,128)(2,1)S(1)}, u32[]{:S(2)}, u32[]{:S(2)}) collective-permute-start(bf16[2,3,2048]{2,0,1:T(2,128)(2,1)S(1)} %slice.53), channel_id=1, source_target_pairs={{0,8},{8,16},{16,24},{24,32},{32,40},{40,48},{48,56},{56,64},{64,7... | collective-permute-start | bytes 73736 | tf_op jit(solution)/shard_map/ppermute | solution.py:15
  18.1 44.8 %copy-start.4 = (s32[512]{0:T(512)}, s32[512]{0:T(512)S(1)}, u32[]{:S(2)}) copy-start(s32[512]{0:T(512)S(1)} %multiply_add_fusion.2) | copy-start | bytes 6148
  57.3 4.5 copy-start
  65.9 205.4 %all-to-all-start = ((bf16[512,16,128]{0,2,1:T(8,128)(2,1)}), bf16[512,16,128]{0,2,1:T(8,128)(2,1)S(1)}, u32[]{:S(2)}, u32[]{:S(2)}) async-start(bf16[512,16,128]{0,2,1:T(8,128)(2,1)} %select_convert_fusion), calls=%async_computation | async-start | bytes 4194304 | tf_op jit(solution)/shard_map/all_to_all | solution.py:163
  271.3 1.3 copy-start.3
  299.4 35.1 %copy-start.2 = (f32[128,128,128]{2,0,1:T(8,128)}, f32[128,128,128]{2,0,1:T(8,128)S(1)}, u32[]{:S(2)}) copy-start(f32[128,128,128]{2,0,1:T(8,128)S(1)} %get-tuple-element.265) | copy-start | bytes 25165828
  380.0 11.7 %copy-start.1 = (f32[128,128,128]{2,1,0:T(8,128)S(1)}, f32[128,128,128]{2,1,0:T(8,128)}, u32[]{:S(2)}) copy-start(f32[128,128,128]{2,1,0:T(8,128)} %get-tuple-element.262) | copy-start | bytes 25165828
  505.8 66.0 %copy-start.5 = (s32[512]{0:T(512)S(1)}, s32[512]{0:T(512)}, u32[]{:S(2)}) copy-start(s32[512]{0:T(512)} %copy-done.4) | copy-start | bytes 6148
  505.8 66.0 %copy-start.6 = (f32[2048]{0:T(1024)S(1)}, f32[2048]{0:T(1024)}, u32[]{:S(2)}) copy-start(f32[2048]{0:T(1024)} %param.13) | copy-start | bytes 24580
  505.8 60.5 %all-to-all-start.1 = ((f32[16,512,128]{2,1,0:T(8,128)}), f32[16,512,128]{2,1,0:T(8,128)}, u32[]{:S(2)}, u32[]{:S(2)}) async-start(f32[16,512,128]{2,1,0:T(8,128)} %bitcast_dynamic-update-slice_fusion), calls=%async_computation.1 | async-start | bytes 8388608 | tf_op jit(solution)/shard_map/all_to_all | solution.py:169
  513.2 144.7 %reduce-scatter.2.cloned.1.call-start = ((), (), s32[]{:S(2)}) async-start(), calls=%async_computation.3 | async-start | bytes 6291456 | tf_op jit(solution)/shard_map/reduce_scatter | solution.py:173
Sparse Core Ops, SparseCore 0:
  593.1 64.7 reduce-scatter.1
